TPU v7x, 32 devices: a whole 2x2x4 slice. The times are simulated.
32 devices in a mesh: section: 4 (over z), seq: 4 (over y, x), tp: 2 (over core).
Axes of the slice: x: 2, y: 2, z: 4, core: 2. Of those that a mesh axis runs over, the one named last changes fastest.
Arguments:
- queries: bfloat16 [4, 1024, 8192], P('section', 'seq', 'tp'), may hold values from -300 to 300
- vision: bfloat16 [128, 7680], P(('section', 'tp'), 'seq'), may hold values from -6 to 6
- kv_weight: bfloat16 [4, 7680, 2048], P('section', 'seq', 'tp'), may hold values from -0.0625 to 0.0625
- key_gain: float32 [4, 128], P('section'), may hold values from 0.25 to 1.75
- head_gate: float32 [4, 64], P('section', 'tp'), may hold values from -1.5 to 1.5
Outputs:
- attended: bfloat16 [4, 1024, 8192], P('section', 'seq', 'tp')
All inputs are finite; a program needn't handle non-finite values.
Results may differ from a plain program's by a relative error of at most 0.01.
The roundings to bfloat16 on the way count: a program that leaves them out, or rounds other values in their place, can miss the bound.
Values may be sent and summed in bfloat16 or wider, within the bound.
A program may use at most 64 MiB of HBM per device.

v0:
```python
import math

import jax
import jax.numpy as jnp
from jax import lax
from jax.sharding import PartitionSpec as P

eps_norm = 1e-05


def normalize(projected, gain, head_dim):
    rows = projected.shape[0]
    shaped = projected.reshape(rows, -1, 2, head_dim)
    keys_raw = shaped[:, :, 0]
    values_raw = shaped[:, :, 1]
    scaled = (
        keys_raw
        * lax.rsqrt(jnp.mean(keys_raw * keys_raw, axis=-1, keepdims=True) + eps_norm)
        * gain
    )
    return (scaled.astype(jnp.bfloat16), values_raw.astype(jnp.bfloat16))


def fold_keys(carry, grouped, keys, values):
    rows = keys.shape[0]
    block = math.gcd(rows, 128)
    key_blocks = keys.reshape(rows // block, block, keys.shape[1], keys.shape[2])
    value_blocks = values.reshape(rows // block, block, values.shape[1], values.shape[2])
    scale = grouped.shape[-1] ** (-0.5)

    def advance(state, blocks):
        running_max, running_sum, weighted = state
        key_block, value_block = blocks
        scores = (
            jnp.einsum("tigd,rid->tigr", grouped, key_block, preferred_element_type=jnp.float32)
            * scale
        )
        new_max = jnp.maximum(running_max, jnp.max(scores, axis=-1))
        factor = jnp.exp(running_max - new_max)
        exp_scores = jnp.exp(scores - new_max[..., None])
        running_sum = running_sum * factor + jnp.sum(exp_scores, axis=-1)
        weighted = weighted * factor[..., None] + jnp.einsum(
            "tigr,rid->tigd",
            exp_scores.astype(jnp.bfloat16),
            value_block,
            preferred_element_type=jnp.float32,
        )
        return ((new_max, running_sum, weighted), None)

    state, unused = lax.scan(advance, carry, (key_blocks, value_blocks))
    return state


def local(queries, vision, kv_weight, key_gain, head_gate):
    local_weight = kv_weight[0]
    head_dim = key_gain.shape[1]
    partials = jnp.dot(
        lax.all_gather(vision, ("section", "tp"), axis=0, tiled=True),
        local_weight,
        preferred_element_type=jnp.float32,
    )
    tokens = queries.shape[1]
    pair_heads = local_weight.shape[1] // (2 * head_dim)
    query_heads = head_gate.shape[1]
    group = query_heads // pair_heads
    grouped = queries[0].reshape(tokens, pair_heads, group, head_dim)
    initial = (
        jnp.full((tokens, pair_heads, group), -1e30, jnp.float32),
        jnp.zeros((tokens, pair_heads, group), jnp.float32),
        jnp.zeros((tokens, pair_heads, group, head_dim), jnp.float32),
    )
    shares = lax.psum_scatter(partials, "seq", scatter_dimension=0, tiled=True)
    keys, values = normalize(shares, key_gain[0], head_dim)
    state = fold_keys(
        initial,
        grouped,
        lax.all_gather(keys, "seq", axis=0, tiled=True),
        lax.all_gather(values, "seq", axis=0, tiled=True),
    )
    running_max, running_sum, weighted = state
    gate = jnp.tanh(head_gate[0]).reshape(1, pair_heads, group, 1)
    result = weighted / running_sum[..., None] * gate
    return result.reshape(1, tokens, query_heads * head_dim).astype(jnp.bfloat16)


def solution(mesh):
    return jax.shard_map(
        local,
        mesh=mesh,
        in_specs=(
            P("section", "seq", "tp"),
            P(("section", "tp"), "seq"),
            P("section", "seq", "tp"),
            P("section", None),
            P("section", "tp"),
        ),
        out_specs=P("section", "seq", "tp"),
        check_vma=False,
    )
```

profile of v0, /device:TPU:0, one launch (start us, length us, event | category | flops | bytes accessed | tf_op | source)
XLA Modules:
  0.0 88.3 jit_solution(7843838622367598786)
XLA Ops:
  6.5 0.0 reduce-scatter.2.cloned.1.call-start
  6.5 16.7 %all_gather.9 = bf16[128,1920]{1,0:T(8,128)(2,1)S(1)} all-gather(bf16[16,1920]{1,0:T(8,128)(2,1)} %param.6), channel_id=1, replica_groups=mesh['section'=4,'seq'=4,'tp'=2] {'section','tp'}, dimensions={0}, use_global_device_ids=true | all-gather | bytes 552960 | tf_op jit(solution)/shard_map/all_gather | solution.py:58
  23.2 0.0 copy-start.2
  23.3 0.0 copy-start.1
  23.3 3.6 %fusion.4 = f32[128,1024]{1,0:T(8,128)} fusion(bf16[128,1920]{1,0:T(8,128)(2,1)S(1)} %all_gather.9, bf16[1,1920,1024]{2,1,0:T(8,128)(2,1)} %param.7), kind=kOutput, calls=%fused_computation.7 | convolution fusion | flops 503316480 | bytes 4947968 | tf_op jit(solution)/shard_map/dot_general | solution.py:57
  26.9 0.0 reduce-scatter.2.cloned.1.call-update
  26.9 2.1 %copy.22 = bf16[32,8,32,128]{3,2,1,0:T(8,128)(2,1)S(1)} copy(bf16[32,8,32,128]{3,1,2,0:T(8,128)(2,1)} %bitcast.48) | data formatting | bytes 4194304
  29.0 0.0 copy-done.2
  29.0 0.1 tanh.11
  29.1 24.1 %reduce-scatter.2.cloned.1.call-done = f32[32,1024]{1,0:T(8,128)} async-done(((f32[128,1024]{1,0:T(8,128)}), f32[32,1024]{1,0:T(8,128)}) %reduce-scatter.2.cloned.1.call-update) | async-done | bytes 131088 | tf_op jit(solution)/shard_map/reduce_scatter | solution.py:72
  53.2 1.0 %reshape.53 = f32[32,4,2,128]{3,2,1,0:T(2,128)S(1)} reshape(f32[32,1024]{1,0:T(8,128)} %reduce-scatter.2.cloned.1.call-done) | data formatting | bytes 262144 | tf_op jit(solution)/shard_map/reshape | solution.py:13
  54.3 0.1 slice.10
  54.4 0.1 multiply_reduce_fusion
  54.5 0.0 copy-done.1
  54.5 0.1 multiply_convert_fusion
  54.6 8.6 %all_gather.10 = bf16[128,4,128]{2,0,1:T(8,128)(2,1)S(1)} all-gather(bf16[32,4,128]{2,0,1:T(8,128)(2,1)S(1)} %multiply_convert_fusion), channel_id=1, replica_groups=mesh['section'=4,'seq'=4,'tp'=2] {'seq'}, dimensions={0}, use_global_device_ids=true | all-gather | bytes 163840 | tf_op jit(solution)/shard_map/all_gather | solution.py:77
  63.2 1.5 %bitcast_reduce_fusion = (f32[256,4,8]{0,2,1:T(8,128)S(1)}, f32[4,128,256,8]{2,1,3,0:T(8,128)S(1)}) fusion(bf16[256,4,8,128]{3,2,1,0:T(8,128)(2,1)S(1)} %bitcast.47, bf16[128,4,128]{2,0,1:T(8,128)(2,1)S(1)} %all_gather.10), kind=kOutput, calls=%fused_computation.5 | convolution fusion | flops 270524416 | bytes 6455296 | tf_op jit(solution)/shard_map/while/body/eval_jaxpr/tigd,rid->tigr/dot_general | solution.py:35
  64.7 0.0 copy-start
  64.7 1.9 %copy-done = f32[4,128,256,8]{2,1,3,0:T(8,128)} copy-done((f32[4,128,256,8]{2,1,3,0:T(8,128)}, f32[4,128,256,8]{2,1,3,0:T(8,128)S(1)}, u32[]{:S(2)}) %copy-start) | copy-done | bytes 4194328
  66.6 0.8 fusion.6
  67.5 7.3 %all-gather = bf16[128,4,1,128]{3,1,2,0:T(4,128)(2,1)S(1)} all-gather(bf16[32,4,1,128]{3,1,2,0:T(4,128)(2,1)S(1)} %copy.31), channel_id=2, replica_groups=mesh['section'=4,'seq'=4,'tp'=2] {'seq'}, dimensions={0}, use_global_device_ids=true | all-gather | bytes 163840 | tf_op jit(solution)/shard_map/all_gather | solution.py:78
  74.8 0.1 copy.14
  75.0 3.6 %fusion.2 = bf16[256,4,8,128]{0,3,2,1:T(8,128)(2,1)S(1)} fusion(f32[4,128,256,8]{2,1,3,0:T(8,128)} %copy-done, f32[4,8]{1,0:T(4,128)S(1)} %tanh.11, f32[256,4,8]{0,2,1:T(8,128)S(1)} %get-tuple-element.18, f32[256,4,8]{0,2,1:T(8,128)S(1)} %broadcast_maximum_fusion, f32[256,4,8]{0,2,1:T(8,128)S(1)} %get-tuple-element.17, bf16[128,4,1,128]{0,3,1,2:T(8,128)(2,1)S(1)} %copy.14), kind=kOutput, calls=%fused_computation.3 | convolution fusion | flops 275775488 | bytes 6520960 | tf_op jit(solution)/shard_map/while/body/eval_jaxpr/tigr,rid->tigd/dot_general | solution.py:42
  78.5 2.9 %copy.16 = bf16[1,256,4096]{2,1,0:T(8,128)(2,1)} copy(bf16[1,256,4096]{1,2,0:T(8,128)(2,1)S(1)} %bitcast.49) | data formatting | bytes 4194304 | tf_op jit(solution)/shard_map/convert_element_type | solution.py:83
  (6 shorter events, 0.1 us)
Async XLA Ops:
  6.5 46.7 %reduce-scatter.2.cloned.1.call-start = ((), (), s32[]{:S(2)}) async-start(), calls=%async_computation.1 | async-start | bytes 655360 | tf_op jit(solution)/shard_map/reduce_scatter | solution.py:72
  23.2 5.8 %copy-start.2 = (f32[1,32]{1,0:T(1,128)S(1)}, f32[1,32]{1,0:T(1,128)}, u32[]{:S(2)}) copy-start(f32[1,32]{1,0:T(1,128)} %param.9) | copy-start | bytes 388
  23.3 31.3 %copy-start.1 = (f32[1,128]{1,0:T(1,128)S(1)}, f32[1,128]{1,0:T(1,128)}, u32[]{:S(2)}) copy-start(f32[1,128]{1,0:T(1,128)} %param.8) | copy-start | bytes 1540
  64.7 1.9 %copy-start = (f32[4,128,256,8]{2,1,3,0:T(8,128)}, f32[4,128,256,8]{2,1,3,0:T(8,128)S(1)}, u32[]{:S(2)}) copy-start(f32[4,128,256,8]{2,1,3,0:T(8,128)S(1)} %get-tuple-element.20) | copy-start | bytes 12582916
Sparse Core Ops, SparseCore 0:
  27.0 26.1 reduce-scatter.1
where the time goes:
time: 88.5 us; the launch traced here: 88.3 us
  blocking collectives  32.6 us (37%)
  waiting for transfers between devices  24.1 us (27%)
  between operations  13.5 us (15%)
  matrix products  8.73 us (10%)
  local copies, waits for them, and re-layouts  8.23 us (9%)
  other arithmetic  1.01 us (1%)
    reduce_scatter x1, waiting for transfers between devices, local(): shares = lax.psum_scatter(partials, 'seq', scatter_dimension=0, tiled=True)  24.1 us
    all_gather x1, blocking collectives, local(): lax.all_gather(vision, ('section', 'tp'), axis=0, tiled=True)  16.7 us
    all_gather x1, blocking collectives, local(): lax.all_gather(keys, 'seq', axis=0, tiled=True)  8.61 us
    all_gather x1, blocking collectives, local(): lax.all_gather(values, 'seq', axis=0, tiled=True)  7.32 us
    unnamed x8, local copies, waits for them, and re-layouts  3.99 us
    dot_general x1, matrix products, local(): jnp.dot(lax.all_gather(vision, ('section', 'tp'), axis=0, tiled=True), lo...  3.65 us
    dot_general x1, matrix products, advance(): jnp.einsum('tigr,rid->tigd', exp_scores.astype(jnp.bfloat16), value_block...  3.58 us
    convert_element_type x1, local copies, waits for them, and re-layouts, local(): result.reshape(1, tokens, query_heads * head_dim).astype(jnp.bfloat16)  2.86 us
  transfers between devices with their start and end apart: 1, of which 1 were waited for; matrix products, arithmetic and copies ran while one was open for 2% of the time, Pallas kernels for 0%

commit v1 on v0

v1 whole, which is shorter than its diff:
```python
import functools

import jax
import jax.numpy as jnp
from jax import lax
from jax.experimental import pallas as pl
from jax.experimental.pallas import tpu as pltpu
from jax.sharding import PartitionSpec as P

MESH = pl.DeviceIdType.MESH
eps_norm = 1e-05


def project_kernel(
    sizes,
    head_dim,
    vision_ref,
    weight_ref,
    gain_ref,
    out_ref,
    seen,
    weights,
    partial,
    landed,
    ready,
    gathered,
    weight_sem,
    far_send,
    pass_send,
    seen_sem,
    sum_send,
    sum_recv,
    kv_send,
    kv_recv,
):
    n_s, n_q, n_t = sizes
    s, q, t = lax.axis_index("section"), lax.axis_index("seq"), lax.axis_index("tp")
    stages = partial.shape[0]
    half = n_s // stages
    share = partial.shape[2]
    columns = partial.shape[3]
    base = (s // half) * half

    load = pltpu.make_async_copy(weight_ref.at[0], weights, weight_sem)
    load.start()

    def section_of(stage, j):
        return lax.rem(base + stage * half, n_s) + lax.rem(s + j, half)

    others_s = [section_of(k // half, k % half) for k in range(1, n_s)]
    others_q = [lax.rem(q + k, n_q) for k in range(1, n_q)]
    others_t = [lax.rem(t + k, n_t) for k in range(1, n_t)]

    barrier = pltpu.get_barrier_semaphore()
    peers = (
        [(s, q, o) for o in others_t]
        + [(o, q, t) for o in others_s]
        + [(s, o, t) for o in others_q]
    )
    for peer in peers:
        pl.semaphore_signal(barrier, inc=1, device_id=peer, device_id_type=MESH)
    pl.semaphore_wait(barrier, len(peers))

    mine = s * n_t + t
    sent = []

    def send(src, dst, send_sem, recv_sem, peer):
        copy = pltpu.make_async_remote_copy(
            src_ref=src,
            dst_ref=dst,
            send_sem=send_sem,
            recv_sem=recv_sem,
            device_id=peer,
            device_id_type=MESH,
        )
        copy.start()
        sent.append(copy)

    def arrived(dst, sem):
        pltpu.make_async_copy(dst, dst, sem).wait()

    for k, o in enumerate(others_t):
        send(vision_ref, seen.at[mine], pass_send.at[k], seen_sem.at[mine], (s, q, o))
    for k, o in enumerate(others_s):
        send(vision_ref, seen.at[mine], far_send.at[k], seen_sem.at[mine], (o, q, t))
    seen[mine] = vision_ref[...]
    load.wait()

    for stage in range(stages):
        first = lax.rem(base + stage * half, n_s)
        for j in range(half):
            o = section_of(stage, j)
            slot = o * n_t + t
            if stage * half + j > 0:
                arrived(seen.at[slot], seen_sem.at[slot])
                for k, p in enumerate(others_t):
                    send(
                        seen.at[slot],
                        seen.at[slot],
                        pass_send.at[(stage * half + j) * (n_t - 1) + k],
                        seen_sem.at[slot],
                        (s, q, p),
                    )
        for j in range(half):
            o = section_of(stage, j)
            for p in others_t:
                slot = o * n_t + p
                arrived(seen.at[slot], seen_sem.at[slot])
        block = seen[pl.ds(first * n_t, half * n_t)]
        block = block.reshape(block.shape[0] * block.shape[1], block.shape[2])
        width = 2 * head_dim
        for c in range(columns // width):
            at = slice(c * width, (c + 1) * width)
            product = jnp.dot(block, weights[:, at], preferred_element_type=jnp.float32)
            partial[stage, :, :, at] = product.reshape(n_q, share, width)
        for k, o in enumerate(others_q):
            send(
                partial.at[stage, o],
                landed.at[stage, k],
                sum_send.at[stage, k],
                sum_recv.at[stage, k],
                (s, o, t),
            )

    for stage in range(stages):
        for k in range(n_q - 1):
            arrived(landed.at[stage, k], sum_recv.at[stage, k])
        for h in range(columns // (2 * head_dim)):
            at_k = slice(2 * h * head_dim, (2 * h + 1) * head_dim)
            at_v = slice((2 * h + 1) * head_dim, (2 * h + 2) * head_dim)
            raw_k = partial[stage, q, :, at_k]
            raw_v = partial[stage, q, :, at_v]
            for k in range(n_q - 1):
                raw_k += landed[stage, k, :, at_k]
                raw_v += landed[stage, k, :, at_v]
            mean = jnp.mean(raw_k * raw_k, axis=-1, keepdims=True)
            scaled = raw_k * lax.rsqrt(mean + eps_norm) * gain_ref[...]
            ready[stage, :, at_k] = scaled.astype(jnp.bfloat16)
            ready[stage, :, at_v] = raw_v.astype(jnp.bfloat16)
        for k, o in enumerate(others_q):
            send(
                ready.at[stage],
                gathered.at[stage, q],
                kv_send.at[stage, k],
                kv_recv.at[stage, q],
                (s, o, t),
            )
        gathered[stage, q] = ready[stage]

    for stage in range(stages):
        for o in others_q:
            arrived(gathered.at[stage, o], kv_recv.at[stage, o])
    out_ref[...] = gathered[...].reshape(out_ref.shape)
    for copy in sent:
        copy.wait_send()


def attend_kernel(head_dim, group, pair, q_ref, kv_ref, gate_ref, out_ref):
    head = pl.program_id(0)
    keys = kv_ref[:, :head_dim]
    values = kv_ref[:, head_dim:]
    rows = keys.shape[0]
    tokens = q_ref.shape[1]
    scale = head_dim ** (-0.5)
    if pair == 2:
        zero = jnp.zeros_like(keys)
        keys = jnp.concatenate(
            [jnp.concatenate([keys, zero], 1), jnp.concatenate([zero, keys], 1)], 0
        )
        values = jnp.concatenate(
            [jnp.concatenate([values, zero], 1), jnp.concatenate([zero, values], 1)], 0
        )
    for g in range(0, group, pair):
        at = slice(g * head_dim, (g + pair) * head_dim)
        scores = lax.dot_general(
            q_ref[0, :, at], keys, (((1,), (1,)), ((), ())), preferred_element_type=jnp.float32
        )
        exps, factors = [], []
        for p in range(pair):
            part = scores[:, p * rows : (p + 1) * rows]
            peak = jnp.max(part, axis=-1, keepdims=True)
            exp_scores = jnp.exp((part - peak) * scale)
            total = jnp.sum(exp_scores, axis=-1, keepdims=True)
            gate = jnp.tanh(jnp.full((1, head_dim), gate_ref[0, head * group + g + p]))
            factors.append(gate / jnp.broadcast_to(total, (tokens, head_dim)))
            exps.append(exp_scores.astype(jnp.bfloat16))
        exps = exps[0] if pair == 1 else jnp.concatenate(exps, 1)
        factors = factors[0] if pair == 1 else jnp.concatenate(factors, 1)
        mixed = jnp.dot(exps, values, preferred_element_type=jnp.float32)
        out_ref[0, :, at] = (mixed * factors).astype(jnp.bfloat16)


def local(sizes, queries, vision, kv_weight, key_gain, head_gate):
    n_s, n_q, n_t = sizes
    head_dim = key_gain.shape[1]
    shard, features = vision.shape
    columns = kv_weight.shape[2]
    rows = shard * n_s * n_t
    stages = 2 if n_s % 2 == 0 and rows % (32 * n_q) == 0 else 1
    share = rows // (stages * n_q)
    vmem = pl.BlockSpec(memory_space=pltpu.VMEM)
    dma = pltpu.SemaphoreType.DMA
    key_values = pl.pallas_call(
        functools.partial(project_kernel, sizes, head_dim),
        out_shape=jax.ShapeDtypeStruct((rows, columns), jnp.bfloat16),
        in_specs=[vmem, pl.BlockSpec(memory_space=pl.ANY), vmem],
        out_specs=vmem,
        scratch_shapes=[
            pltpu.VMEM((n_s * n_t, shard, features), jnp.bfloat16),
            pltpu.VMEM((features, columns), jnp.bfloat16),
            pltpu.VMEM((stages, n_q, share, columns), jnp.float32),
            pltpu.VMEM((stages, n_q - 1, share, columns), jnp.float32),
            pltpu.VMEM((stages, share, columns), jnp.bfloat16),
            pltpu.VMEM((stages, n_q, share, columns), jnp.bfloat16),
            dma,
            dma((n_s - 1,)),
            dma((n_s * (n_t - 1),)),
            dma((n_s * n_t,)),
            dma((stages, n_q - 1)),
            dma((stages, n_q - 1)),
            dma((stages, n_q - 1)),
            dma((stages, n_q)),
        ],
        compiler_params=pltpu.CompilerParams(collective_id=0, has_side_effects=True),
        name="project",
    )(vision, kv_weight, key_gain)

    tokens = queries.shape[1]
    pair_heads = columns // (2 * head_dim)
    group = head_gate.shape[1] // pair_heads
    pair = 2 if group % 2 == 0 and rows == head_dim else 1
    wide = group * head_dim
    return pl.pallas_call(
        functools.partial(attend_kernel, head_dim, group, pair),
        out_shape=jax.ShapeDtypeStruct(queries.shape, jnp.bfloat16),
        grid=(pair_heads,),
        in_specs=[
            pl.BlockSpec((1, tokens, wide), lambda i: (0, 0, i)),
            pl.BlockSpec((rows, 2 * head_dim), lambda i: (0, i)),
            pl.BlockSpec(memory_space=pltpu.SMEM),
        ],
        out_specs=pl.BlockSpec((1, tokens, wide), lambda i: (0, 0, i)),
        name="attend",
    )(queries, key_values, head_gate)


def solution(mesh):
    sizes = tuple(mesh.shape[name] for name in ("section", "seq", "tp"))
    return jax.shard_map(
        functools.partial(local, sizes),
        mesh=mesh,
        in_specs=(
            P("section", "seq", "tp"),
            P(("section", "tp"), "seq"),
            P("section", "seq", "tp"),
            P("section", None),
            P("section", "tp"),
        ),
        out_specs=P("section", "seq", "tp"),
        check_vma=False,
    )
```

time: 88.5 us -> 30.4 us (0.34)
  blocking collectives: 32.6 us -> 0 us
  Pallas kernels: 0 us -> 30.1 us
  waiting for transfers between devices: 24.1 us -> 0 us
  between operations: 13.5 us -> 0.01 us
  matrix products: 8.73 us -> 0 us
  local copies, waits for them, and re-layouts: 8.23 us -> 0 us
  other arithmetic: 1.01 us -> 0 us
    all_gather x3 -> x0, blocking collectives: 32.6 us -> none  [the longest x1 16.7 us: local(): lax.all_gather(vision, ('section', 'tp'), axis=0, tiled=True)]
    pallas_call x0 -> x2, Pallas kernels: none -> 30.1 us  [the longest x1 24 us: local(): pl.pallas_call(functools.partial(project_kernel, sizes, head_dim), out_sh...]
    reduce_scatter x1 -> x0, waiting for transfers between devices: 24.1 us -> none  [local(): shares = lax.psum_scatter(partials, 'seq', scatter_dimension=0, tiled=True)]
    dot_general x3 -> x0, matrix products: 8.73 us -> none  [the longest x1 3.65 us: local(): jnp.dot(lax.all_gather(vision, ('section', 'tp'), axis=0, tiled=True), lo...]
    unnamed x8 -> x0, local copies, waits for them, and re-layouts: 3.99 us -> none
    convert_element_type x1 -> x0, local copies, waits for them, and re-layouts: 2.86 us -> none  [local(): result.reshape(1, tokens, query_heads * head_dim).astype(jnp.bfloat16)]
    reshape x1 -> x0, local copies, waits for them, and re-layouts: 1.02 us -> none  [normalize(): shaped = projected.reshape(rows, -1, 2, head_dim)]
    reduce_sum x2 -> x0, other arithmetic: 0.9 us -> none  [the longest x1 0.81 us: advance(): running_sum = running_sum * factor + jnp.sum(exp_scores, axis=-1)]
  transfers between devices with their start and end apart: 1 -> 0, of which waited for: 1 -> 0; matrix products, arithmetic and copies ran while one was open for 2% -> 0% of each run, Pallas kernels for 0% -> 0%
where the time goes in v1:
time: 30.4 us; the launch traced here: 30.2 us
  Pallas kernels  30.1 us (99%)
    pallas_call x1, Pallas kernels, local(): pl.pallas_call(functools.partial(project_kernel, sizes, head_dim), out_sh...  24 us
    pallas_call x1, Pallas kernels, local(): pl.pallas_call(functools.partial(attend_kernel, head_dim, group, pair), o...  6.1 us

profile of v1, /device:TPU:0, one launch (start us, length us, event | category | flops | bytes accessed | tf_op | source)
XLA Modules:
  0.0 30.2 jit_solution(9182591282660261105)
XLA Ops:
  0.0 24.0 %project.1.kv_ref = bf16[128,1024]{1,0:T(8,128)(2,1)} custom-call(bf16[16,1920]{1,0:T(8,128)(2,1)} %vision_ref.1, bf16[1,1920,1024]{2,1,0:T(8,128)(2,1)} %weight_ref.1, f32[1,128]{1,0:T(1,128)} %gain_ref.1), custom_call_target="tpu_custom_call" | custom-call | tf_op jit(solution)/shard_map/project/pallas_call | solution.py:203
  24.1 6.1 %attend.1 = bf16[1,256,4096]{2,1,0:T(8,128)(2,1)} custom-call(bf16[1,256,4096]{2,1,0:T(8,128)(2,1)} %q_ref.1, bf16[128,1024]{1,0:T(8,128)(2,1)} %project.1.kv_ref, f32[1,32]{1,0:T(1,128)} %gate_ref.1), custom_call_target="tpu_custom_call" | custom-call | tf_op jit(solution)/shard_map/attend/pallas_call | solution.py:233

commit v2 on v1

v2 whole, which is shorter than its diff:
```python
import functools

import jax
import jax.numpy as jnp
from jax import lax
from jax.experimental import pallas as pl
from jax.experimental.pallas import tpu as pltpu
from jax.sharding import PartitionSpec as P

MESH = pl.DeviceIdType.MESH
eps_norm = 1e-05


def project_kernel(
    sizes,
    head_dim,
    vision_ref,
    weight_ref,
    gain_ref,
    query_ref,
    key_ref,
    value_ref,
    staged_ref,
    seen,
    weights,
    gain,
    partial,
    landed,
    ready,
    gathered,
    load_sem,
    far_send,
    pass_send,
    seen_sem,
    sum_send,
    sum_recv,
    kv_send,
    kv_recv,
):
    n_s, n_q, n_t = sizes
    s, q, t = lax.axis_index("section"), lax.axis_index("seq"), lax.axis_index("tp")
    stages = partial.shape[0]
    per = n_s // stages
    half = n_s // 2 if n_s % 2 == 0 else n_s
    share = partial.shape[2]
    columns = partial.shape[3]
    heads = columns // (2 * head_dim)
    base = (s // half) * half

    def section_of(k):
        return lax.rem(base + (k // half) * half, n_s) + lax.rem(s + k, half)

    def place_at(k):
        return (k // half) * half + (half - k % half) % half

    others_s = [section_of(k) for k in range(1, n_s)]
    others_q = [lax.rem(q + k, n_q) for k in range(1, n_q)]
    others_t = [lax.rem(t + k, n_t) for k in range(1, n_t)]

    barrier = pltpu.get_barrier_semaphore()
    peers = (
        [(o, q, t) for o in others_s[::-1]]
        + [(s, o, t) for o in others_q]
        + [(s, q, o) for o in others_t]
    )
    for peer in peers:
        pl.semaphore_signal(barrier, inc=1, device_id=peer, device_id_type=MESH)
    own = pltpu.make_async_copy(vision_ref, seen.at[0, t], load_sem.at[0])
    own.start()
    load = pltpu.make_async_copy(weight_ref.at[0], weights, load_sem.at[1])
    load.start()
    load_gain = pltpu.make_async_copy(gain_ref, gain, load_sem.at[2])
    load_gain.start()
    stage_queries = pltpu.make_async_copy(query_ref, staged_ref, load_sem.at[3])
    stage_queries.start()
    own.wait()
    pl.semaphore_wait(barrier, len(peers))

    sent = []

    def send(src, dst, send_sem, recv_sem, peer):
        copy = pltpu.make_async_remote_copy(
            src_ref=src,
            dst_ref=dst,
            send_sem=send_sem,
            recv_sem=recv_sem,
            device_id=peer,
            device_id_type=MESH,
        )
        copy.start()
        sent.append(copy)

    def arrived(dst, sem):
        pltpu.make_async_copy(dst, dst, sem).wait()

    def pass_on(k):
        for i, o in enumerate(others_t):
            send(seen.at[k, t], seen.at[k, t], pass_send.at[k, i], seen_sem.at[k, t], (s, q, o))

    pass_on(0)
    for k, o in enumerate(others_s, 1):
        place = place_at(k)
        send(
            seen.at[0, t], seen.at[place, t], far_send.at[k - 1], seen_sem.at[place, t], (o, q, t)
        )
    load_gain.wait()
    load.wait()

    def project(stage):
        for k in range(stage * per, (stage + 1) * per):
            if k > 0:
                arrived(seen.at[k, t], seen_sem.at[k, t])
                pass_on(k)
        for k in range(stage * per, (stage + 1) * per):
            for o in others_t:
                arrived(seen.at[k, o], seen_sem.at[k, o])
        block = seen[stage * per : (stage + 1) * per]
        block = block.reshape(n_q * share, block.shape[3])
        width = 2 * head_dim
        for h in range(heads):
            at = slice(h * width, (h + 1) * width)
            product = jnp.dot(block, weights[:, at], preferred_element_type=jnp.float32)
            partial[stage, :, :, at] = product.reshape(n_q, share, width)
        for k, o in enumerate(others_q):
            send(
                partial.at[stage, o],
                landed.at[stage, k],
                sum_send.at[stage, k],
                sum_recv.at[stage, k],
                (s, o, t),
            )

    def finish(stage):
        for k in range(n_q - 1):
            arrived(landed.at[stage, k], sum_recv.at[stage, k])
        for h in range(heads):
            at_k = slice(2 * h * head_dim, (2 * h + 1) * head_dim)
            at_v = slice((2 * h + 1) * head_dim, (2 * h + 2) * head_dim)
            raw_k = partial[stage, q, :, at_k]
            raw_v = partial[stage, q, :, at_v]
            for k in range(n_q - 1):
                raw_k += landed[stage, k, :, at_k]
                raw_v += landed[stage, k, :, at_v]
            mean = jnp.mean(raw_k * raw_k, axis=-1, keepdims=True)
            scaled = raw_k * lax.rsqrt(mean + eps_norm) * gain[...]
            both = jnp.concatenate([scaled, raw_v], axis=0).astype(jnp.bfloat16)
            ready[stage, :, h * head_dim : (h + 1) * head_dim] = both
        for k, o in enumerate(others_q):
            send(
                ready.at[stage],
                gathered.at[stage, q],
                kv_send.at[stage, k],
                kv_recv.at[stage, q],
                (s, o, t),
            )
        gathered[stage, q] = ready[stage]

    def collect(stage):
        for o in others_q:
            arrived(gathered.at[stage, o], kv_recv.at[stage, o])
        block = gathered[stage].astype(jnp.float32)
        at = slice(stage * n_q * share, (stage + 1) * n_q * share)
        shape = (n_q * share, heads * head_dim)
        key_ref[at, :] = block[:, :share].reshape(shape).astype(jnp.bfloat16)
        value_ref[at, :] = block[:, share:].reshape(shape).astype(jnp.bfloat16)

    for stage in range(stages):
        project(stage)
        if stage >= 2:
            finish(stage - 2)
    for stage in range(max(stages - 2, 0), stages):
        finish(stage)
    for stage in range(stages):
        collect(stage)
    stage_queries.wait()
    for copy in sent:
        copy.wait_send()


def attend_kernel(head_dim, group, pair, q_ref, k_ref, v_ref, gate_ref, out_ref):
    head = pl.program_id(0)
    at_head = pl.ds(pl.multiple_of(head * head_dim, head_dim), head_dim)
    keys = k_ref[:, at_head]
    values = v_ref[:, at_head]
    rows = keys.shape[0]
    scale = head_dim ** (-0.5)
    ones = jnp.ones((rows, head_dim), jnp.bfloat16)

    def diagonal(block):
        if pair == 1:
            return block
        zero = jnp.zeros_like(block)
        return jnp.concatenate(
            [jnp.concatenate([block, zero], 1), jnp.concatenate([zero, block], 1)], 0
        )

    keys, values, ones = diagonal(keys), diagonal(values), diagonal(ones)
    wide = pair * head_dim
    tokens = q_ref.shape[1]
    tile = tokens // 1
    units = [(g, r) for g in range(0, group, pair) for r in range(0, tokens, tile)]

    def score(g, r):
        start = pl.multiple_of(head * (group * head_dim) + g * head_dim, wide)
        return lax.dot_general(
            q_ref[0, r : r + tile, pl.ds(start, wide)],
            keys,
            (((1,), (1,)), ((), ())),
            preferred_element_type=jnp.float32,
        )

    def soften(scores):
        exps = []
        for p in range(pair):
            part = scores[:, p * rows : (p + 1) * rows]
            peak = jnp.max(part, axis=-1, keepdims=True)
            exps.append(jnp.exp((part - peak) * scale).astype(jnp.bfloat16))
        return exps[0] if pair == 1 else jnp.concatenate(exps, 1)

    def mix(exps, g, r):
        gates = [
            jnp.full((1, head_dim), gate_ref[0, head * group + g + p]) for p in range(pair)
        ]
        gates = gates[0] if pair == 1 else jnp.concatenate(gates, 1)
        mixed = jnp.dot(exps, values, preferred_element_type=jnp.float32)
        total = jnp.dot(exps, ones, preferred_element_type=jnp.float32)
        result = mixed / total * jnp.tanh(gates)
        out_ref[0, r : r + tile, g * head_dim : g * head_dim + wide] = result.astype(jnp.bfloat16)

    depth = 1
    waiting_scores, waiting_exps = [], []
    for step in range(len(units) + 2 * depth):
        if step < len(units):
            waiting_scores.append(score(*units[step]))
        if depth <= step < len(units) + depth:
            waiting_exps.append(soften(waiting_scores.pop(0)))
        if step >= 2 * depth:
            mix(waiting_exps.pop(0), *units[step - 2 * depth])


def local(sizes, queries, vision, kv_weight, key_gain, head_gate):
    n_s, n_q, n_t = sizes
    head_dim = key_gain.shape[1]
    shard, features = vision.shape
    columns = kv_weight.shape[2]
    rows = shard * n_s * n_t
    stages = 1
    for tried in (2, 4):
        if n_s % tried == 0 and rows % (tried * 8 * n_q) == 0:
            stages = tried
    share = rows // (stages * n_q)
    hbm = pl.BlockSpec(memory_space=pltpu.HBM)
    vmem = pl.BlockSpec(memory_space=pltpu.VMEM)
    dma = pltpu.SemaphoreType.DMA
    keys, values, staged = pl.pallas_call(
        functools.partial(project_kernel, sizes, head_dim),
        out_shape=(
            pltpu.VMEM((rows, columns // 2), jnp.bfloat16),
            pltpu.VMEM((rows, columns // 2), jnp.bfloat16),
            pltpu.VMEM(queries.shape, jnp.bfloat16),
        ),
        in_specs=[hbm, hbm, hbm, hbm],
        out_specs=(vmem, vmem, vmem),
        scratch_shapes=[
            pltpu.VMEM((n_s, n_t, shard, features), jnp.bfloat16),
            pltpu.VMEM((features, columns), jnp.bfloat16),
            pltpu.VMEM(key_gain.shape, jnp.float32),
            pltpu.VMEM((stages, n_q, share, columns), jnp.float32),
            pltpu.VMEM((stages, n_q - 1, share, columns), jnp.float32),
            pltpu.VMEM((stages, 2 * share, columns // 2), jnp.bfloat16),
            pltpu.VMEM((stages, n_q, 2 * share, columns // 2), jnp.bfloat16),
            dma((4,)),
            dma((n_s - 1,)),
            dma((n_s, n_t - 1)),
            dma((n_s, n_t)),
            dma((stages, n_q - 1)),
            dma((stages, n_q - 1)),
            dma((stages, n_q - 1)),
            dma((stages, n_q)),
        ],
        compiler_params=pltpu.CompilerParams(
            collective_id=0, has_side_effects=True, vmem_limit_bytes=24 << 20
        ),
        name="project",
    )(*[pltpu.with_memory_space_constraint(x, pltpu.HBM) for x in (vision, kv_weight, key_gain, queries)])

    tokens = queries.shape[1]
    pair_heads = columns // (2 * head_dim)
    group = head_gate.shape[1] // pair_heads
    pair = 2 if group % 2 == 0 and rows == head_dim else 1
    wide = group * head_dim
    return pl.pallas_call(
        functools.partial(attend_kernel, head_dim, group, pair),
        out_shape=jax.ShapeDtypeStruct(queries.shape, jnp.bfloat16),
        grid=(pair_heads,),
        in_specs=[vmem, vmem, vmem, pl.BlockSpec(memory_space=pltpu.SMEM)],
        out_specs=pl.BlockSpec((1, tokens, wide), lambda i: (0, 0, i)),
        compiler_params=pltpu.CompilerParams(vmem_limit_bytes=24 << 20),
        name="attend",
    )(staged, keys, values, head_gate)


def solution(mesh):
    sizes = tuple(mesh.shape[name] for name in ("section", "seq", "tp"))
    return jax.shard_map(
        functools.partial(local, sizes),
        mesh=mesh,
        in_specs=(
            P("section", "seq", "tp"),
            P(("section", "tp"), "seq"),
            P("section", "seq", "tp"),
            P("section", None),
            P("section", "tp"),
        ),
        out_specs=P("section", "seq", "tp"),
        check_vma=False,
    )
```

time: 30.4 us -> 27.7 us (0.911)
  Pallas kernels: 30.1 us -> 27.6 us
    pallas_call x1, Pallas kernels: 6.1 us -> 4.66 us  [local(): pl.pallas_call(functools.partial(attend_kernel, head_dim, group, pair), o...]
    pallas_call x1, Pallas kernels: 24 us -> 22.9 us  [local(): pl.pallas_call(functools.partial(project_kernel, sizes, head_dim), out_sh...]
where the time goes in v2:
time: 27.7 us; the launch traced here: 27.6 us
  Pallas kernels  27.6 us (100%)
    pallas_call x1, Pallas kernels, local(): pl.pallas_call(functools.partial(project_kernel, sizes, head_dim), out_sh...  22.9 us
    pallas_call x1, Pallas kernels, local(): pl.pallas_call(functools.partial(attend_kernel, head_dim, group, pair), o...  4.66 us

profile of v2, /device:TPU:0, one launch (start us, length us, event | category | flops | bytes accessed | tf_op | source)
XLA Modules:
  0.0 27.6 jit_solution(12772515175920749398)
XLA Ops:
  0.0 0.0 copy-start
  0.0 22.9 %project.1 = (bf16[128,512]{1,0:T(8,128)(2,1)S(1)}, bf16[128,512]{1,0:T(8,128)(2,1)S(1)}, bf16[1,256,4096]{2,1,0:T(8,128)(2,1)S(1)}) custom-call(bf16[16,1920]{1,0:T(8,128)(2,1)} %vision_ref.1, bf16[1,1920,1024]{2,1,0:T(8,128)(2,1)} %weight_ref.1, f32[1,128]{1,0:T(1,128)} %gain_ref.1, bf16[1,256,4096]{2,1,0:T(8,128)(2,1)} %query_ref.1), custom_call_target="tpu_custom_call" | custom-call | tf_op jit(solution)/shard_map/project/pallas_call | solution.py:255
  22.9 0.0 copy-done
  22.9 4.7 %attend.1 = bf16[1,256,4096]{2,1,0:T(8,128)(2,1)} custom-call(bf16[1,256,4096]{2,1,0:T(8,128)(2,1)S(1)} %get-tuple-element.8.q_ref, bf16[128,512]{1,0:T(8,128)(2,1)S(1)} %get-tuple-element.9.k_ref, bf16[128,512]{1,0:T(8,128)(2,1)S(1)} %get-tuple-element.10.v_ref, f32[1,32]{1,0:T(1,128)S(1)} %copy-done), custom_call_target="tpu_custom_call" | custom-call | tf_op jit(solution)/shard_map/attend/pallas_call | solution.py:292
Async XLA Ops:
  0.0 22.9 %copy-start = (f32[1,32]{1,0:T(1,128)S(1)}, f32[1,32]{1,0:T(1,128)}, u32[]{:S(2)}) copy-start(f32[1,32]{1,0:T(1,128)} %gate_ref.1) | copy-start | bytes 388

commit v3 on v2

--- a/solution.py
+++ b/solution.py
@@ -177,12 +177,9 @@
         copy.wait_send()
 
 
-def attend_kernel(head_dim, group, pair, q_ref, k_ref, v_ref, gate_ref, out_ref):
-    head = pl.program_id(0)
-    at_head = pl.ds(pl.multiple_of(head * head_dim, head_dim), head_dim)
-    keys = k_ref[:, at_head]
-    values = v_ref[:, at_head]
-    rows = keys.shape[0]
+def attend_kernel(head_dim, group, pair, many, q_ref, k_ref, v_ref, gate_ref, out_ref):
+    first = pl.program_id(0) * many
+    rows = k_ref.shape[0]
     scale = head_dim ** (-0.5)
     ones = jnp.ones((rows, head_dim), jnp.bfloat16)
 
@@ -194,17 +191,21 @@
             [jnp.concatenate([block, zero], 1), jnp.concatenate([zero, block], 1)], 0
         )
 
-    keys, values, ones = diagonal(keys), diagonal(values), diagonal(ones)
+    keys, values, ones = [], [], diagonal(ones)
+    for i in range(many):
+        at = pl.ds(pl.multiple_of((first + i) * head_dim, head_dim), head_dim)
+        keys.append(diagonal(k_ref[:, at]))
+        values.append(diagonal(v_ref[:, at]))
     wide = pair * head_dim
     tokens = q_ref.shape[1]
     tile = tokens // 1
-    units = [(g, r) for g in range(0, group, pair) for r in range(0, tokens, tile)]
+    units = [(g, r) for g in range(0, many * group, pair) for r in range(0, tokens, tile)]
 
     def score(g, r):
-        start = pl.multiple_of(head * (group * head_dim) + g * head_dim, wide)
+        start = pl.multiple_of(first * (group * head_dim) + g * head_dim, wide)
         return lax.dot_general(
             q_ref[0, r : r + tile, pl.ds(start, wide)],
-            keys,
+            keys[g // group],
             (((1,), (1,)), ((), ())),
             preferred_element_type=jnp.float32,
         )
@@ -219,15 +220,15 @@
 
     def mix(exps, g, r):
         gates = [
-            jnp.full((1, head_dim), gate_ref[0, head * group + g + p]) for p in range(pair)
+            jnp.full((1, head_dim), gate_ref[0, first * group + g + p]) for p in range(pair)
         ]
         gates = gates[0] if pair == 1 else jnp.concatenate(gates, 1)
-        mixed = jnp.dot(exps, values, preferred_element_type=jnp.float32)
+        mixed = jnp.dot(exps, values[g // group], preferred_element_type=jnp.float32)
         total = jnp.dot(exps, ones, preferred_element_type=jnp.float32)
         result = mixed / total * jnp.tanh(gates)
         out_ref[0, r : r + tile, g * head_dim : g * head_dim + wide] = result.astype(jnp.bfloat16)
 
-    depth = 1
+    depth = 2
     waiting_scores, waiting_exps = [], []
     for step in range(len(units) + 2 * depth):
         if step < len(units):
@@ -288,11 +289,12 @@
     pair_heads = columns // (2 * head_dim)
     group = head_gate.shape[1] // pair_heads
     pair = 2 if group % 2 == 0 and rows == head_dim else 1
-    wide = group * head_dim
+    many = 2 if pair_heads % 4 == 0 else 1
+    wide = many * group * head_dim
     return pl.pallas_call(
-        functools.partial(attend_kernel, head_dim, group, pair),
+        functools.partial(attend_kernel, head_dim, group, pair, many),
         out_shape=jax.ShapeDtypeStruct(queries.shape, jnp.bfloat16),
-        grid=(pair_heads,),
+        grid=(pair_heads // many,),
         in_specs=[vmem, vmem, vmem, pl.BlockSpec(memory_space=pltpu.SMEM)],
         out_specs=pl.BlockSpec((1, tokens, wide), lambda i: (0, 0, i)),
         compiler_params=pltpu.CompilerParams(vmem_limit_bytes=24 << 20),

time: 27.7 us -> 27 us (0.975)
  Pallas kernels: 27.6 us -> 26.8 us
    pallas_call x1, Pallas kernels: 4.66 us -> 3.92 us  [local(): pl.pallas_call(functools.partial(attend_kernel, head_dim, group, pair, ma...]
where the time goes in v3:
time: 27 us; the launch traced here: 26.8 us
  Pallas kernels  26.8 us (99%)
    pallas_call x1, Pallas kernels, local(): pl.pallas_call(functools.partial(project_kernel, sizes, head_dim), out_sh...  22.9 us
    pallas_call x1, Pallas kernels, local(): pl.pallas_call(functools.partial(attend_kernel, head_dim, group, pair, ma...  3.92 us

profile of v3, /device:TPU:0, one launch (start us, length us, event | category | flops | bytes accessed | tf_op | source)
XLA Modules:
  0.0 26.8 jit_solution(1676928754926619730)
XLA Ops:
  0.0 0.0 copy-start
  0.0 22.9 %project.1 = (bf16[128,512]{1,0:T(8,128)(2,1)S(1)}, bf16[128,512]{1,0:T(8,128)(2,1)S(1)}, bf16[1,256,4096]{2,1,0:T(8,128)(2,1)S(1)}) custom-call(bf16[16,1920]{1,0:T(8,128)(2,1)} %vision_ref.1, bf16[1,1920,1024]{2,1,0:T(8,128)(2,1)} %weight_ref.1, f32[1,128]{1,0:T(1,128)} %gain_ref.1, bf16[1,256,4096]{2,1,0:T(8,128)(2,1)} %query_ref.1), custom_call_target="tpu_custom_call" | custom-call | tf_op jit(solution)/shard_map/project/pallas_call | solution.py:256
  22.9 0.0 copy-done
  22.9 3.9 %attend.1 = bf16[1,256,4096]{2,1,0:T(8,128)(2,1)} custom-call(bf16[1,256,4096]{2,1,0:T(8,128)(2,1)S(1)} %get-tuple-element.8.q_ref, bf16[128,512]{1,0:T(8,128)(2,1)S(1)} %get-tuple-element.9.k_ref, bf16[128,512]{1,0:T(8,128)(2,1)S(1)} %get-tuple-element.10.v_ref, f32[1,32]{1,0:T(1,128)S(1)} %copy-done), custom_call_target="tpu_custom_call" | custom-call | tf_op jit(solution)/shard_map/attend/pallas_call | solution.py:294
Async XLA Ops:
  0.0 22.9 %copy-start = (f32[1,32]{1,0:T(1,128)S(1)}, f32[1,32]{1,0:T(1,128)}, u32[]{:S(2)}) copy-start(f32[1,32]{1,0:T(1,128)} %gate_ref.1) | copy-start | bytes 388
